TPU v7x, 32 devices: a whole 2x2x4 slice. The times are simulated.
32 devices in a mesh: seq: 4 (over y, x), exp: 8 (over z, core).
Axes of the slice: x: 2, y: 2, z: 4, core: 2. Of those that a mesh axis runs over, the one named last changes fastest.
Arguments:
- inputs: bfloat16 [4096, 4096], P(('seq', 'exp')), may hold values from -6 to 6
- queries: bfloat16 [4096, 4096], P(('seq', 'exp')), may hold values from -40 to 40
- keys: bfloat16 [4096, 4096], P(('seq', 'exp')), may hold values from -4 to 4
- values: bfloat16 [4096, 4096], P(('seq', 'exp')), may hold values from -6 to 6
- norm_gain: float32 [4096], replicated, may hold values from 0.25 to 1.75
- expert_ids: int32 [4096, 2], P(('seq', 'exp')), may hold values from 0 to 7, all different within a row; in each aligned block of 128 rows (0 to 127, 128 to 255, ...) at most 32 rows name the same one
- gate_weights: float32 [4096, 2], P(('seq', 'exp')), may hold values from 0.2 to 1
- pairs: int32 [16, 2], replicated, may hold values from 0 to 7, as said below
- w_gate: bfloat16 [8, 4096, 4096], P('exp', None, 'seq'), may hold values from -0.09375 to 0.09375
- w_up: bfloat16 [8, 4096, 4096], P('exp', None, 'seq'), may hold values from -0.09375 to 0.09375
- w_down: bfloat16 [8, 4096, 4096], P('exp', 'seq'), may hold values from -0.09375 to 0.09375
Outputs:
- output: bfloat16 [4096, 4096], P(('seq', 'exp'))
Inputs may be any that keep to these rules, and one draw needn't show every extreme that they name: `pairs`: each row is (query block, key block) with the key block from the query block - 2 to the query block; rows are distinct; every block is paired with itself; some pair has distance 2. `expert_ids`: the 2 ids of a token differ; within the 128 rows of one device every expert is named exactly 32 times.
All inputs are finite; a program needn't handle non-finite values.
Results may differ from a plain program's by a relative error of at most 0.007.
Values may be sent and summed in bfloat16 or wider, within the bound.
A program may use at most 128 MiB of HBM per device.

v0:
```python
import math
import jax
import jax.numpy as jnp
from jax import lax
from jax.sharding import PartitionSpec as P

HSZ = 128
TOP = 2
BLK = 512
DIST = 2
very_negative = -1e30
norm_epsilon = 1e-05


def from_behind(value, axis, steps):
    count = lax.axis_size(axis)
    leading, last = (max(0, -steps), min(count, count - steps))
    return lax.ppermute(value, axis, [(source, source + steps) for source in range(leading, last)])


def expert_part(flat_rows, gate_slice, up_slice, down_slice):
    gate_value = jnp.dot(flat_rows, gate_slice, preferred_element_type=jnp.float32)
    up_value = jnp.dot(flat_rows, up_slice, preferred_element_type=jnp.float32)
    hidden = (jax.nn.silu(gate_value) * up_value).astype(jnp.bfloat16)
    return jnp.dot(hidden, down_slice, preferred_element_type=jnp.float32)


def block_present(pairs, query_block, distance):
    matches = (pairs[:, 0] == query_block) & (pairs[:, 1] == query_block - distance)
    return jnp.any(matches)


def per_device(
    inputs, queries, keys, values, norm_gain, expert_ids, gate_weights, pairs, w_gate, w_up, w_down
):
    rows_dev, model_width = inputs.shape
    exp_count = lax.axis_size("exp")
    score_scale = 1.0 / math.sqrt(HSZ)
    query_run, key_run, value_run = (
        lax.all_to_all(queries, "exp", split_axis=1, concat_axis=0, tiled=True),
        lax.all_to_all(keys, "exp", split_axis=1, concat_axis=0, tiled=True),
        lax.all_to_all(values, "exp", split_axis=1, concat_axis=0, tiled=True),
    )
    run_rows, group_width = query_run.shape
    heads_dev = group_width // HSZ
    tail_rows = DIST * BLK
    keys_prev, values_prev = from_behind(
        (key_run[run_rows - tail_rows :], value_run[run_rows - tail_rows :]), "seq", 1
    )
    keys_ext = jnp.concatenate([keys_prev, key_run], 0).reshape(-1, heads_dev, HSZ)
    values_ext = jnp.concatenate([values_prev, value_run], 0).reshape(-1, heads_dev, HSZ)
    blocks_dev = run_rows // BLK
    first_block = lax.axis_index("seq") * blocks_dev
    attended_blocks = []
    for local_block in range(blocks_dev):
        query_block = first_block + local_block
        query_rows = query_run[local_block * BLK : (local_block + 1) * BLK].reshape(
            BLK, heads_dev, HSZ
        )
        present = [
            block_present(pairs, query_block, DIST - key_slot) for key_slot in range(DIST + 1)
        ]
        window_start = tail_rows + (local_block - DIST) * BLK
        window_end = window_start + (DIST + 1) * BLK
        scores = (
            jnp.einsum(
                "qhd,khd->hqk",
                query_rows,
                keys_ext[window_start:window_end],
                preferred_element_type=jnp.float32,
            )
            * score_scale
        )
        key_mask = jnp.repeat(jnp.stack(present), BLK)
        scores = jnp.where(key_mask[None, None, :], scores, very_negative)
        row_top = jnp.max(scores, axis=2, keepdims=True)
        exp_scores = jnp.exp(scores - row_top)
        denominator = jnp.sum(exp_scores, axis=2)
        weights = exp_scores.astype(jnp.bfloat16)
        summed = jnp.einsum(
            "hqk,khd->qhd",
            weights,
            values_ext[window_start:window_end],
            preferred_element_type=jnp.float32,
        )
        attended_block = (summed / jnp.transpose(denominator)[:, :, None]).astype(jnp.bfloat16)
        attended_blocks.append(attended_block.reshape(BLK, group_width))
    attended_run = jnp.concatenate(attended_blocks, 0)
    attended = lax.all_to_all(attended_run, "exp", split_axis=0, concat_axis=1, tiled=True)
    mixed_sum = inputs.astype(jnp.float32) + attended.astype(jnp.float32)
    mean_square = jnp.mean(mixed_sum * mixed_sum, axis=1, keepdims=True)
    normed = (mixed_sum * lax.rsqrt(mean_square + norm_epsilon) * norm_gain[None, :]).astype(
        jnp.bfloat16
    )
    capacity = rows_dev * TOP // exp_count
    flat_ids = expert_ids.reshape(-1)
    assignments = flat_ids.shape[0]
    id_table = (flat_ids[:, None] == jnp.arange(exp_count, dtype=jnp.int32)[None, :]).astype(
        jnp.int32
    )
    ahead_count = jnp.cumsum(id_table, axis=0) - id_table
    position = jnp.sum(ahead_count * id_table, axis=1)
    target = flat_ids * capacity + position
    source = (
        jnp.zeros((exp_count * capacity,), jnp.int32)
        .at[target]
        .set(jnp.arange(assignments, dtype=jnp.int32))
    )
    outgoing = normed[source // TOP].reshape(exp_count, capacity, model_width)
    gate_slice = w_gate[0]
    up_slice = w_up[0]
    down_slice = w_down[0]
    piece_rows = lax.all_gather(
        lax.all_to_all(outgoing, "exp", split_axis=0, concat_axis=0, tiled=True),
        "seq",
        axis=0,
        tiled=True,
    )
    flat_rows = piece_rows.reshape(-1, model_width)
    slice_parts = expert_part(flat_rows, gate_slice, up_slice, down_slice).reshape(piece_rows.shape)
    slice_total = lax.psum_scatter(
        slice_parts.astype(jnp.bfloat16), "seq", scatter_dimension=0, tiled=True
    ).astype(jnp.float32)
    expert_out = lax.all_to_all(
        slice_total.astype(jnp.bfloat16), "exp", split_axis=0, concat_axis=0, tiled=True
    ).astype(slice_total.dtype)
    gathered = expert_out.reshape(exp_count * capacity, model_width)[target].reshape(
        rows_dev, TOP, model_width
    )
    output = mixed_sum + jnp.sum(gate_weights[:, :, None] * gathered, axis=1)
    return output.astype(jnp.bfloat16)


def solution(mesh):
    in_specs = (
        P(("seq", "exp"), None),
        P(("seq", "exp"), None),
        P(("seq", "exp"), None),
        P(("seq", "exp"), None),
        P(),
        P(("seq", "exp"), None),
        P(("seq", "exp"), None),
        P(),
        P("exp", None, "seq"),
        P("exp", None, "seq"),
        P("exp", "seq", None),
    )
    out_specs = P(("seq", "exp"), None)
    return jax.shard_map(
        per_device, mesh=mesh, in_specs=in_specs, out_specs=out_specs, check_vma=False
    )
```

profile of v0, /device:TPU:0, one launch (start us, length us, event | category | flops | bytes accessed | tf_op | source)
XLA Modules:
  0.0 532.3 jit_solution(13733365971950306756)
XLA Ops:
  9.6 6.4 %all-to-all-start = ((bf16[128,8,512]{2,0,1:T(8,128)(2,1)}), bf16[128,8,512]{2,0,1:T(8,128)(2,1)S(1)}, u32[]{:S(2)}, u32[]{:S(2)}) async-start(bf16[128,8,512]{2,0,1:T(8,128)(2,1)} %copy.69), calls=%async_computation | async-start | bytes 2097152 | tf_op jit(solution)/shard_map/all_to_all | solution.py:42
  17.3 25.2 %all-to-all-done = bf16[128,8,512]{2,0,1:T(8,128)(2,1)S(1)} async-done(((bf16[128,8,512]{2,0,1:T(8,128)(2,1)}), bf16[128,8,512]{2,0,1:T(8,128)(2,1)S(1)}, u32[]{:S(2)}, u32[]{:S(2)}) %all-to-all-start) | async-done | bytes 1048608 | tf_op jit(solution)/shard_map/all_to_all | solution.py:42
  42.5 3.7 all-to-all-start.1
  48.5 24.2 %all-to-all-done.1 = bf16[128,8,512]{0,2,1:T(8,128)(2,1)S(1)} async-done(((bf16[128,8,512]{0,2,1:T(8,128)(2,1)}), bf16[128,8,512]{0,2,1:T(8,128)(2,1)S(1)}, u32[]{:S(2)}, u32[]{:S(2)}) %all-to-all-start.1) | async-done | bytes 1048608 | tf_op jit(solution)/shard_map/all_to_all | solution.py:41
  72.7 3.6 all-to-all-start.2
  77.7 4.4 collective-permute-start.1
  91.8 11.0 %all-to-all-done.2 = bf16[128,8,512]{2,0,1:T(8,128)(2,1)S(1)} async-done(((bf16[128,8,512]{2,0,1:T(8,128)(2,1)}), bf16[128,8,512]{2,0,1:T(8,128)(2,1)S(1)}, u32[]{:S(2)}, u32[]{:S(2)}) %all-to-all-start.2) | async-done | bytes 1048608 | tf_op jit(solution)/shard_map/all_to_all | solution.py:40
  109.1 7.3 %bitcast_reduce_fusion = (f32[4,512]{1,0:T(4,128)S(1)}, f32[4,1536,512]{2,1,0:T(8,128)}) fusion(pred[1536]{0:T(1024)(128)(4,1)S(1)} %broadcast_in_dim.46, bf16[1536,4,128]{0,2,1:T(8,128)(2,1)S(1)} %bitcast.108, bf16[512,4,128]{2,1,0:T(4,128)(2,1)} %reshape.135), kind=kOutput, calls=%fused_computation.4 | convolution fusion | flops 814741504 | bytes 14689792 | tf_op jit(solution)/shard_map/qhd,khd->hqk/dot_general | solution.py:66
  117.1 7.0 %fusion.4 = f32[4,512]{1,0:T(4,128)S(1)} fusion(f32[4,1536,512]{2,1,0:T(8,128)} %get-tuple-element.18, f32[4,512]{1,0:T(4,128)S(1)} %get-tuple-element.17, pred[1536]{0:T(1024)(128)(4,1)S(1)} %broadcast_in_dim.46), kind=kLoop, calls=%fused_computation.13 | loop fusion | flops 12580864 | bytes 12600832 | tf_op jit(solution)/shard_map/reduce_sum | solution.py:78
  135.1 3.9 fusion.2
  143.7 4.7 all-to-all-start.3
  151.6 23.4 %all-to-all-done.3 = bf16[8,128,512]{2,1,0:T(8,128)(2,1)S(1)} async-done(((bf16[8,128,512]{2,1,0:T(8,128)(2,1)}), bf16[8,128,512]{2,1,0:T(8,128)(2,1)S(1)}, u32[]{:S(2)}, u32[]{:S(2)}) %all-to-all-start.3) | async-done | bytes 1048608 | tf_op jit(solution)/shard_map/all_to_all | solution.py:89
  180.1 53.4 %all_to_all.77 = bf16[8,32,4096]{2,1,0:T(8,128)(2,1)} all-to-all(bf16[8,32,4096]{2,1,0:T(8,128)(2,1)} %bitcast.109), channel_id=1, replica_groups=mesh['seq'=4,'exp'=8] {'exp'}, dimensions={0} | all-to-all | bytes 4194304 | tf_op jit(solution)/shard_map/all_to_all | solution.py:114
  233.6 87.5 %all-gather.2.cloned.1.call-done = bf16[32,32,4096]{2,1,0:T(8,128)(2,1)} async-done(((bf16[8,32,4096]{2,1,0:T(8,128)(2,1)}), bf16[32,32,4096]{2,1,0:T(8,128)(2,1)}) %all-gather.2.cloned.1.call-update) | async-done | bytes 8388624 | tf_op jit(solution)/shard_map/all_gather | solution.py:113
  321.1 12.8 %fusion.8 = f32[1024,1024]{1,0:T(8,128)S(1)} fusion(bf16[1024,4096]{1,0:T(8,128)(2,1)} %bitcast.128, bf16[1,4096,1024]{2,1,0:T(8,128)(2,1)} %param.20), kind=kOutput, calls=%fused_computation.17 | convolution fusion | flops 8589934592 | bytes 20971520 | tf_op jit(solution)/shard_map/dot_general | solution.py:23
  333.9 12.0 %multiply_convert_fusion = bf16[1024,1024]{1,0:T(8,128)(2,1)S(1)} fusion(f32[1024,1024]{1,0:T(8,128)S(1)} %fusion.8, bf16[1024,4096]{1,0:T(8,128)(2,1)S(1)} %bitcast.129, bf16[1,4096,1024]{2,1,0:T(8,128)(2,1)} %param.19), kind=kOutput, calls=%fused_computation.27 | convolution fusion | flops 8596226048 | bytes 23068672 | tf_op jit(solution)/shard_map/dot_general | solution.py:22
  345.9 11.0 %fusion.12 = bf16[32,32,4096]{2,1,0:T(8,128)(2,1)} fusion(bf16[32,32,1024]{2,1,0:T(8,128)(2,1)S(1)} %bitcast.130, bf16[1,1024,4096]{2,1,0:T(8,128)(2,1)S(1)} %bitcast.127), kind=kOutput, calls=%fused_computation.21 | convolution fusion | flops 8594128896 | bytes 18874368 | tf_op jit(solution)/shard_map/dot_general | solution.py:25
  356.9 86.5 %reduce-scatter.2.cloned.1.call-done = bf16[8,32,4096]{2,1,0:T(8,128)(2,1)} async-done(((bf16[32,32,4096]{2,1,0:T(8,128)(2,1)}), bf16[8,32,4096]{2,1,0:T(8,128)(2,1)}) %reduce-scatter.2.cloned.1.call-update) | async-done | bytes 2097168 | tf_op jit(solution)/shard_map/reduce_scatter | solution.py:121
  443.4 4.9 all-to-all-start.5
  448.4 48.9 %all-to-all-done.5 = bf16[8,32,4096]{2,1,0:T(8,128)(2,1)} async-done(((bf16[8,32,4096]{2,1,0:T(8,128)(2,1)}), bf16[8,32,4096]{2,1,0:T(8,128)(2,1)}, u32[]{:S(2)}, u32[]{:S(2)}) %all-to-all-start.5) | async-done | bytes 2097184 | tf_op jit(solution)/shard_map/all_to_all | solution.py:124
  497.4 4.0 bitcast_convert_fusion
  501.4 7.8 %gather_fusion.1 = f32[256,4096]{1,0:T(8,128)} fusion(f32[256,4096]{1,0:T(8,128)} %bitcast_convert_fusion, s32[1024]{0:T(1024)S(1)} %pad_clamp_fusion), kind=kCustom, calls=%fused_computation.1 | custom fusion | bytes 8389632 | tf_op jit(solution)/shard_map/gather | solution.py:127
  509.2 5.8 %reshape.142 = f32[128,2,4096]{2,1,0:T(2,128)} reshape(f32[256,4096]{1,0:T(8,128)} %gather_fusion.1) | data formatting | bytes 8388608 | tf_op jit(solution)/shard_map/reshape | solution.py:127
  515.0 8.8 %multiply_reduce_fusion = f32[128,4096]{1,0:T(8,128)S(1)} fusion(f32[128,2,4096]{2,1,0:T(2,128)} %reshape.142, f32[128,2]{1,0:T(8,128)S(1)} %copy.85), kind=kLoop, calls=%fused_computation.26 | loop fusion | flops 1572864 | bytes 6292480 | tf_op jit(solution)/shard_map/reduce_sum | solution.py:130
  (87 shorter events, 50.2 us)
Async XLA Ops:
  6.5 9.4 %copy-start.6 = (bf16[128,4096]{1,0:T(8,128)(2,1)S(1)}, bf16[128,4096]{1,0:T(8,128)(2,1)}, u32[]{:S(2)}) copy-start(bf16[128,4096]{1,0:T(8,128)(2,1)} %param.13) | copy-start | bytes 3145732
  9.6 32.9 %all-to-all-start = ((bf16[128,8,512]{2,0,1:T(8,128)(2,1)}), bf16[128,8,512]{2,0,1:T(8,128)(2,1)S(1)}, u32[]{:S(2)}, u32[]{:S(2)}) async-start(bf16[128,8,512]{2,0,1:T(8,128)(2,1)} %copy.69), calls=%async_computation | async-start | bytes 2097152 | tf_op jit(solution)/shard_map/all_to_all | solution.py:42
  42.5 39.6 %copy-start.10 = (s32[16,2]{0,1:T(2,128)S(1)}, s32[16,2]{0,1:T(2,128)}, u32[]{:S(2)}) copy-start(s32[16,2]{0,1:T(2,128)} %param.18) | copy-start | bytes 388
  42.5 30.2 %all-to-all-start.1 = ((bf16[128,8,512]{0,2,1:T(8,128)(2,1)}), bf16[128,8,512]{0,2,1:T(8,128)(2,1)S(1)}, u32[]{:S(2)}, u32[]{:S(2)}) async-start(bf16[128,8,512]{0,2,1:T(8,128)(2,1)} %bitcast.8), calls=%async_computation.1 | async-start | bytes 2097152 | tf_op jit(solution)/shard_map/all_to_all | solution.py:41
  72.7 3.6 copy-start.4
  72.7 30.1 %all-to-all-start.2 = ((bf16[128,8,512]{2,0,1:T(8,128)(2,1)}), bf16[128,8,512]{2,0,1:T(8,128)(2,1)S(1)}, u32[]{:S(2)}, u32[]{:S(2)}) async-start(bf16[128,8,512]{2,0,1:T(8,128)(2,1)} %bitcast.103), calls=%async_computation.2 | async-start | bytes 2097152 | tf_op jit(solution)/shard_map/all_to_all | solution.py:40
  77.7 26.9 %collective-permute-start.1 = (bf16[1024,512]{1,0:T(8,128)(2,1)S(1)}, bf16[1024,512]{1,0:T(8,128)(2,1)}, u32[]{:S(2)}, u32[]{:S(2)}) collective-permute-start(bf16[1024,512]{1,0:T(8,128)(2,1)S(1)} %bitcast.110), channel_id=1, source_target_pairs={{0,8},{8,16},{16,24},{1,9},{9,17},{17,25},{2,10},{10,18},{18,26},{... | collective-permute-start | bytes 3145736 | tf_op jit(solution)/shard_map/ppermute | solution.py:18
  88.3 38.4 %collective-permute-start = (bf16[1024,512]{0,1:T(8,128)(2,1)}, bf16[1024,512]{0,1:T(8,128)(2,1)}, u32[]{:S(2)}, u32[]{:S(2)}) collective-permute-start(bf16[1024,512]{0,1:T(8,128)(2,1)} %copy.70), channel_id=1, source_target_pairs={{0,8},{8,16},{16,24},{1,9},{9,17},{17,25},{2,10},{10,18},{18,26},{... | collective-permute-start | bytes 3145736 | tf_op jit(solution)/shard_map/ppermute | solution.py:18
  117.1 11.7 %copy-start = (f32[4,1536,512]{2,1,0:T(8,128)S(1)}, f32[4,1536,512]{2,1,0:T(8,128)}, u32[]{:S(2)}) copy-start(f32[4,1536,512]{2,1,0:T(8,128)} %get-tuple-element.18) | copy-start | bytes 37748740
  128.9 3.2 copy-start.5
  142.2 6.3 %copy-start.8 = (s32[128,2]{0,1:T(2,128)S(1)}, s32[128,2]{0,1:T(2,128)}, u32[]{:S(2)}) copy-start(s32[128,2]{0,1:T(2,128)} %param.16) | copy-start | bytes 3076
  143.7 31.3 %all-to-all-start.3 = ((bf16[8,128,512]{2,1,0:T(8,128)(2,1)}), bf16[8,128,512]{2,1,0:T(8,128)(2,1)S(1)}, u32[]{:S(2)}, u32[]{:S(2)}) async-start(bf16[8,128,512]{2,1,0:T(8,128)(2,1)} %bitcast.26), calls=%async_computation.3 | async-start | bytes 2097152 | tf_op jit(solution)/shard_map/all_to_all | solution.py:89
  148.4 27.1 %copy-start.1 = (bf16[128,4096]{1,0:T(8,128)(2,1)S(1)}, bf16[128,4096]{1,0:T(8,128)(2,1)}, u32[]{:S(2)}) copy-start(bf16[128,4096]{1,0:T(8,128)(2,1)} %param.11) | copy-start | bytes 3145732
  148.4 172.6 %all-gather.2.cloned.1.call-start = ((), (), s32[]{:S(2)}) async-start(), calls=%async_computation.7 | async-start | bytes 10485760 | tf_op jit(solution)/shard_map/all_gather | solution.py:113
  175.3 1.2 copy-start.2
  175.3 1.2 copy-start.7
  233.5 209.9 %reduce-scatter.2.cloned.1.call-start = ((), (), s32[]{:S(2)}) async-start(), calls=%async_computation.8 | async-start | bytes 10485760 | tf_op jit(solution)/shard_map/reduce_scatter | solution.py:121
  321.1 12.9 %copy-start.11 = (bf16[32,32,4096]{2,1,0:T(8,128)(2,1)S(1)}, bf16[32,32,4096]{2,1,0:T(8,128)(2,1)}, u32[]{:S(2)}) copy-start(bf16[32,32,4096]{2,1,0:T(8,128)(2,1)} %all-gather.2.cloned.1.call-done) | copy-start | bytes 25165828
  321.1 24.8 %slice-start = ((s8[8388608]{0:T(1024)(128)(4,1)}), s8[4194304]{0:T(1024)(128)(4,1)S(1)}, s32[]{:S(2)}) async-start(s8[8388608]{0:T(1024)(128)(4,1)} %bitcast.126), calls=%async_computation.9 | async-start | bytes 8388608
  333.9 12.0 %slice-start.1 = ((s8[8388608]{0:T(1024)(128)(4,1)}), s8[4194304]{0:T(1024)(128)(4,1)S(1)}, s32[]{:S(2)}) async-start(s8[8388608]{0:T(1024)(128)(4,1)} %bitcast.126), calls=%async_computation.10 | async-start | bytes 8388608
  356.9 91.4 %copy-start.9 = (f32[128,2]{0,1:T(2,128)S(1)}, f32[128,2]{0,1:T(2,128)}, u32[]{:S(2)}) copy-start(f32[128,2]{0,1:T(2,128)} %param.17) | copy-start | bytes 3076
  443.4 54.0 %all-to-all-start.5 = ((bf16[8,32,4096]{2,1,0:T(8,128)(2,1)}), bf16[8,32,4096]{2,1,0:T(8,128)(2,1)}, u32[]{:S(2)}, u32[]{:S(2)}) async-start(bf16[8,32,4096]{2,1,0:T(8,128)(2,1)} %reduce-scatter.2.cloned.1.call-done), calls=%async_computation.6 | async-start | bytes 4194304 | tf_op jit(solution)/shard_map/all_to_all | solution.py:124
  515.0 8.8 %copy-start.3 = (bf16[128,4096]{1,0:T(8,128)(2,1)S(1)}, bf16[128,4096]{1,0:T(8,128)(2,1)}, u32[]{:S(2)}) copy-start(bf16[128,4096]{1,0:T(8,128)(2,1)} %param.11) | copy-start | bytes 3145732
Sparse Core Ops, SparseCore 0:
  233.6 87.3 all-gather.1
  357.1 86.3 reduce-scatter.1
where the time goes:
time: 543 us; the launch traced here: 532 us
  waiting for transfers between devices  309 us (57%)
  blocking collectives  53.4 us (10%)
  matrix products  52.4 us (10%)
  other arithmetic  36.6 us (7%)
  local copies, waits for them, and re-layouts  35.4 us (7%)
  starting transfers between devices  31.2 us (6%)
  between operations  14 us (3%)
    all_gather x1, waiting for transfers between devices, per_device(): lax.all_gather(lax.all_to_all(outgoing, 'exp', split_axis=0, concat_axis=...  87.5 us
    reduce_scatter x1, waiting for transfers between devices, per_device(): lax.psum_scatter(slice_parts.astype(jnp.bfloat16), 'seq', scatter_dimensi...  86.5 us
    all_to_all x1, blocking collectives, per_device(): lax.all_to_all(outgoing, 'exp', split_axis=0, concat_axis=0, tiled=True)  53.4 us
    all_to_all x1, waiting for transfers between devices, per_device(): lax.all_to_all(slice_total.astype(jnp.bfloat16), 'exp', split_axis=0, con...  48.9 us
    all_to_all x1, waiting for transfers between devices, per_device(): lax.all_to_all(values, 'exp', split_axis=1, concat_axis=0, tiled=True)  25.2 us
    all_to_all x1, waiting for transfers between devices, per_device(): lax.all_to_all(keys, 'exp', split_axis=1, concat_axis=0, tiled=True)  24.2 us
    all_to_all x1, waiting for transfers between devices, per_device(): lax.all_to_all(attended_run, 'exp', split_axis=0, concat_axis=1, tiled=True)  23.4 us
    dot_general x1, matrix products, expert_part(): up_value = jnp.dot(flat_rows, up_slice, preferred_element_type=jnp.float32)  12.8 us
  transfers between devices with their start and end apart: 9, of which 9 were waited for; matrix products, arithmetic and copies ran while one was open for 7% of the time, Pallas kernels for 0%

commit v1 on v0

--- a/solution.py
+++ b/solution.py
@@ -10,6 +10,18 @@
 DIST = 2
 very_negative = -1e30
 norm_epsilon = 1e-05
+
+
+def rotated_exchange(x, axis, split, join):
+    ways, here = (lax.axis_size(axis), lax.axis_index(axis))
+    width = x.shape[split] // ways
+    turned = jnp.roll(x, -here * width, axis=split)
+    got = [lax.slice_in_dim(turned, 0, width, axis=split)]
+    for far in range(1, ways):
+        sent = lax.slice_in_dim(turned, far * width, (far + 1) * width, axis=split)
+        got.append(lax.ppermute(sent, axis, [(d, (d + far) % ways) for d in range(ways)]))
+    line = jnp.concatenate(got[::-1], axis=join)
+    return jnp.roll(line, (here + 1) * got[0].shape[join], axis=join)
 
 
 def from_behind(value, axis, steps):
@@ -38,7 +50,7 @@
     score_scale = 1.0 / math.sqrt(HSZ)
     query_run, key_run, value_run = (
         lax.all_to_all(queries, "exp", split_axis=1, concat_axis=0, tiled=True),
-        lax.all_to_all(keys, "exp", split_axis=1, concat_axis=0, tiled=True),
+        rotated_exchange(keys, "exp", 1, 0),
         lax.all_to_all(values, "exp", split_axis=1, concat_axis=0, tiled=True),
     )
     run_rows, group_width = query_run.shape

time: 543 us -> 553 us (1.018)
  local copies, waits for them, and re-layouts: 35.4 us -> 51.9 us
  waiting for transfers between devices: 309 us -> 301 us
  starting transfers between devices: 31.2 us -> 39 us
    ppermute x0 -> x7, waiting for transfers between devices: none -> 36.5 us  [rotated_exchange(): lax.ppermute(sent, axis, [(d, (d + far) % ways) for d in range(ways)])]
    all_to_all x1, waiting for transfers between devices: 25.2 us -> 0.01 us  [per_device(): lax.all_to_all(values, 'exp', split_axis=1, concat_axis=0, tiled=True)]
    all_to_all x1 -> x0, waiting for transfers between devices: 24.2 us -> none  [per_device(): lax.all_to_all(keys, 'exp', split_axis=1, concat_axis=0, tiled=True)]
    ppermute x2, waiting for transfers between devices: 2.61 us -> 17.8 us  [from_behind(): lax.ppermute(value, axis, [(source, source + steps) for source in range(l...]
    unnamed x32 -> x49, local copies, waits for them, and re-layouts: 3.96 us -> 17.4 us
    ppermute x0 -> x7, starting transfers between devices: none -> 11.7 us  [rotated_exchange(): lax.ppermute(sent, axis, [(d, (d + far) % ways) for d in range(ways)])]
    all_to_all x1, waiting for transfers between devices: 11 us -> 0.01 us  [per_device(): lax.all_to_all(queries, 'exp', split_axis=1, concat_axis=0, tiled=True)]
  transfers between devices with their start and end apart: 9 -> 15, of which waited for: 9 -> 9; matrix products, arithmetic and copies ran while one was open for 7% -> 10% of each run, Pallas kernels for 0% -> 0%
where the time goes in v1:
time: 553 us; the launch traced here: 545 us
  waiting for transfers between devices  301 us (54%)
  blocking collectives  53.4 us (10%)
  local copies, waits for them, and re-layouts  51.9 us (9%)
  matrix products  49.1 us (9%)
  starting transfers between devices  39 us (7%)
  other arithmetic  35.8 us (6%)
  between operations  14.1 us (3%)
    all_gather x1, waiting for transfers between devices, per_device(): lax.all_gather(lax.all_to_all(outgoing, 'exp', split_axis=0, concat_axis=...  88.4 us
    reduce_scatter x1, waiting for transfers between devices, per_device(): lax.psum_scatter(slice_parts.astype(jnp.bfloat16), 'seq', scatter_dimensi...  86.5 us
    all_to_all x1, blocking collectives, per_device(): lax.all_to_all(outgoing, 'exp', split_axis=0, concat_axis=0, tiled=True)  53.4 us
    all_to_all x1, waiting for transfers between devices, per_device(): lax.all_to_all(slice_total.astype(jnp.bfloat16), 'exp', split_axis=0, con...  48.9 us
    ppermute x7, waiting for transfers between devices, rotated_exchange(): lax.ppermute(sent, axis, [(d, (d + far) % ways) for d in range(ways)])  36.5 us
    all_to_all x1, waiting for transfers between devices, per_device(): lax.all_to_all(attended_run, 'exp', split_axis=0, concat_axis=1, tiled=True)  23.3 us
    ppermute x2, waiting for transfers between devices, from_behind(): lax.ppermute(value, axis, [(source, source + steps) for source in range(l...  17.8 us
    unnamed x49, local copies, waits for them, and re-layouts  17.4 us
  transfers between devices with their start and end apart: 15, of which 9 were waited for; matrix products, arithmetic and copies ran while one was open for 10% of the time, Pallas kernels for 0%

profile of v1, /device:TPU:0, one launch (start us, length us, event | category | flops | bytes accessed | tf_op | source)
XLA Modules:
  0.0 544.6 jit_solution(7281737212376796944)
XLA Ops:
  12.8 4.5 collective-permute-start.1
  22.9 3.8 collective-permute-start.2
  31.9 12.1 %collective-permute-done.2 = bf16[128,512]{0,1:T(8,128)(2,1)S(1)} collective-permute-done((bf16[128,512]{0,1:T(8,128)(2,1)}, bf16[128,512]{0,1:T(8,128)(2,1)S(1)}, u32[]{:S(2)}, u32[]{:S(2)}) %collective-permute-start.2) | collective-permute-done | bytes 131104 | tf_op jit(solution)/shard_map/ppermute | solution.py:22
  47.5 22.2 %collective-permute-done.4 = bf16[128,512]{0,1:T(8,128)(2,1)} collective-permute-done((bf16[128,512]{0,1:T(8,128)(2,1)}, bf16[128,512]{0,1:T(8,128)(2,1)}, u32[]{:S(2)}, u32[]{:S(2)}) %collective-permute-start.4) | collective-permute-done | bytes 131104 | tf_op jit(solution)/shard_map/ppermute | solution.py:22
  80.8 4.4 all-to-all-start.1
  87.9 4.4 collective-permute-start.8
  97.1 17.1 %collective-permute-done.8 = bf16[1024,512]{0,1:T(8,128)(2,1)} collective-permute-done((bf16[1024,512]{0,1:T(8,128)(2,1)S(1)}, bf16[1024,512]{0,1:T(8,128)(2,1)}, u32[]{:S(2)}, u32[]{:S(2)}) %collective-permute-start.8) | collective-permute-done | bytes 1048608 | tf_op jit(solution)/shard_map/ppermute | solution.py:30
  118.6 5.5 %collective-permute-start = (bf16[1024,512]{0,1:T(8,128)(2,1)}, bf16[1024,512]{0,1:T(8,128)(2,1)}, u32[]{:S(2)}, u32[]{:S(2)}) collective-permute-start(bf16[1024,512]{0,1:T(8,128)(2,1)} %copy.51), channel_id=1, source_target_pairs={{0,8},{8,16},{16,24},{1,9},{9,17},{17,25},{2,10},{10,18},{18,26},{... | collective-permute-start | bytes 3145736 | tf_op jit(solution)/shard_map/ppermute | solution.py:30
  130.3 4.1 bitcast_reduce_fusion
  134.4 3.9 fusion.4
  155.1 4.5 all-to-all-start.2
  162.9 23.3 %all-to-all-done.2 = bf16[8,128,512]{2,1,0:T(8,128)(2,1)S(1)} async-done(((bf16[8,128,512]{2,1,0:T(8,128)(2,1)}), bf16[8,128,512]{2,1,0:T(8,128)(2,1)S(1)}, u32[]{:S(2)}, u32[]{:S(2)}) %all-to-all-start.2) | async-done | bytes 1048608 | tf_op jit(solution)/shard_map/all_to_all | solution.py:101
  191.7 53.4 %all_to_all.58 = bf16[8,32,4096]{2,1,0:T(8,128)(2,1)} all-to-all(bf16[8,32,4096]{2,1,0:T(8,128)(2,1)} %bitcast.106), channel_id=1, replica_groups=mesh['seq'=4,'exp'=8] {'exp'}, dimensions={0} | all-to-all | bytes 4194304 | tf_op jit(solution)/shard_map/all_to_all | solution.py:126
  245.2 88.4 %all-gather.2.cloned.1.call-done = bf16[32,32,4096]{2,1,0:T(8,128)(2,1)} async-done(((bf16[8,32,4096]{2,1,0:T(8,128)(2,1)}), bf16[32,32,4096]{2,1,0:T(8,128)(2,1)}) %all-gather.2.cloned.1.call-update) | async-done | bytes 8388624 | tf_op jit(solution)/shard_map/all_gather | solution.py:125
  333.6 12.7 %fusion.8 = f32[1024,1024]{1,0:T(8,128)S(1)} fusion(bf16[1024,4096]{1,0:T(8,128)(2,1)} %bitcast.121, bf16[1,4096,1024]{2,1,0:T(8,128)(2,1)} %param.20), kind=kOutput, calls=%fused_computation.17 | convolution fusion | flops 8589934592 | bytes 20971520 | tf_op jit(solution)/shard_map/dot_general | solution.py:35
  346.3 12.0 %multiply_convert_fusion = bf16[1024,1024]{1,0:T(8,128)(2,1)S(1)} fusion(f32[1024,1024]{1,0:T(8,128)S(1)} %fusion.8, bf16[1024,4096]{1,0:T(8,128)(2,1)S(1)} %bitcast.122, bf16[1,4096,1024]{2,1,0:T(8,128)(2,1)} %param.19), kind=kOutput, calls=%fused_computation.27 | convolution fusion | flops 8596226048 | bytes 23068672 | tf_op jit(solution)/shard_map/dot_general | solution.py:34
  358.3 11.0 %fusion.12 = bf16[32,32,4096]{2,1,0:T(8,128)(2,1)} fusion(bf16[32,32,1024]{2,1,0:T(8,128)(2,1)S(1)} %bitcast.123, bf16[1,1024,4096]{2,1,0:T(8,128)(2,1)S(1)} %bitcast.120), kind=kOutput, calls=%fused_computation.21 | convolution fusion | flops 8594128896 | bytes 18874368 | tf_op jit(solution)/shard_map/dot_general | solution.py:37
  369.3 86.5 %reduce-scatter.2.cloned.1.call-done = bf16[8,32,4096]{2,1,0:T(8,128)(2,1)} async-done(((bf16[32,32,4096]{2,1,0:T(8,128)(2,1)}), bf16[8,32,4096]{2,1,0:T(8,128)(2,1)}) %reduce-scatter.2.cloned.1.call-update) | async-done | bytes 2097168 | tf_op jit(solution)/shard_map/reduce_scatter | solution.py:133
  455.8 4.9 all-to-all-start.4
  460.8 48.9 %all-to-all-done.4 = bf16[8,32,4096]{2,1,0:T(8,128)(2,1)} async-done(((bf16[8,32,4096]{2,1,0:T(8,128)(2,1)}), bf16[8,32,4096]{2,1,0:T(8,128)(2,1)}, u32[]{:S(2)}, u32[]{:S(2)}) %all-to-all-start.4) | async-done | bytes 2097184 | tf_op jit(solution)/shard_map/all_to_all | solution.py:136
  509.7 4.0 bitcast_convert_fusion
  513.7 7.8 %gather_fusion.1 = f32[256,4096]{1,0:T(8,128)} fusion(f32[256,4096]{1,0:T(8,128)} %bitcast_convert_fusion, s32[1024]{0:T(1024)S(1)} %pad_clamp_fusion), kind=kCustom, calls=%fused_computation.1 | custom fusion | bytes 8389632 | tf_op jit(solution)/shard_map/gather | solution.py:139
  521.6 5.8 %reshape.139 = f32[128,2,4096]{2,1,0:T(2,128)} reshape(f32[256,4096]{1,0:T(8,128)} %gather_fusion.1) | data formatting | bytes 8388608 | tf_op jit(solution)/shard_map/reshape | solution.py:139
  527.4 8.8 %multiply_reduce_fusion = f32[128,4096]{1,0:T(8,128)S(1)} fusion(f32[128,2,4096]{2,1,0:T(2,128)} %reshape.139, f32[128,2]{1,0:T(8,128)S(1)} %copy.64), kind=kLoop, calls=%fused_computation.26 | loop fusion | flops 1572864 | bytes 6292480 | tf_op jit(solution)/shard_map/reduce_sum | solution.py:142
  (117 shorter events, 76.7 us)
Async XLA Ops:
  8.2 9.2 %copy-start.6 = (bf16[128,4096]{1,0:T(8,128)(2,1)S(1)}, bf16[128,4096]{1,0:T(8,128)(2,1)}, u32[]{:S(2)}) copy-start(bf16[128,4096]{1,0:T(8,128)(2,1)} %param.14) | copy-start | bytes 3145732
  12.8 17.3 %collective-permute-start.1 = (bf16[128,512]{0,1:T(8,128)(2,1)}, bf16[128,512]{0,1:T(8,128)(2,1)S(1)}, u32[]{:S(2)}, u32[]{:S(2)}) collective-permute-start(bf16[128,512]{0,1:T(8,128)(2,1)} %get-tuple-element.23), channel_id=1, source_target_pairs={{0,7},{1,0},{2,1},{3,2},{4,3},{5,4},{6,5},{7,6},{8,15},{9,8},{10,9... | collective-permute-start | bytes 393224 | tf_op jit(solution)/shard_map/ppermute | solution.py:22
  18.0 11.0 %copy-start.7 = (bf16[128,4096]{1,0:T(8,128)(2,1)S(1)}, bf16[128,4096]{1,0:T(8,128)(2,1)}, u32[]{:S(2)}) copy-start(bf16[128,4096]{1,0:T(8,128)(2,1)} %param.12) | copy-start | bytes 3145732
  19.3 61.5 %all-to-all-start = ((bf16[128,8,512]{2,0,1:T(8,128)(2,1)}), bf16[128,8,512]{2,0,1:T(8,128)(2,1)S(1)}, u32[]{:S(2)}, u32[]{:S(2)}) async-start(bf16[128,8,512]{2,0,1:T(8,128)(2,1)} %copy.50), calls=%async_computation | async-start | bytes 2097152 | tf_op jit(solution)/shard_map/all_to_all | solution.py:54
  22.9 21.1 %collective-permute-start.2 = (bf16[128,512]{0,1:T(8,128)(2,1)}, bf16[128,512]{0,1:T(8,128)(2,1)S(1)}, u32[]{:S(2)}, u32[]{:S(2)}) collective-permute-start(bf16[128,512]{0,1:T(8,128)(2,1)} %get-tuple-element.22), channel_id=1, source_target_pairs={{0,6},{1,7},{2,0},{3,1},{4,2},{5,3},{6,4},{7,5},{8,14},{9,15},{10,... | collective-permute-start | bytes 393224 | tf_op jit(solution)/shard_map/ppermute | solution.py:22
  26.6 20.2 %collective-permute-start.3 = (bf16[128,512]{0,1:T(8,128)(2,1)}, bf16[128,512]{0,1:T(8,128)(2,1)S(1)}, u32[]{:S(2)}, u32[]{:S(2)}) collective-permute-start(bf16[128,512]{0,1:T(8,128)(2,1)} %get-tuple-element.21), channel_id=1, source_target_pairs={{0,5},{1,6},{2,7},{3,0},{4,1},{5,2},{6,3},{7,4},{8,13},{9,14},{10,... | collective-permute-start | bytes 393224 | tf_op jit(solution)/shard_map/ppermute | solution.py:22
  26.6 43.1 %collective-permute-start.4 = (bf16[128,512]{0,1:T(8,128)(2,1)}, bf16[128,512]{0,1:T(8,128)(2,1)}, u32[]{:S(2)}, u32[]{:S(2)}) collective-permute-start(bf16[128,512]{0,1:T(8,128)(2,1)} %get-tuple-element.20), channel_id=1, source_target_pairs={{0,4},{1,5},{2,6},{3,7},{4,0},{5,1},{6,2},{7,3},{8,12},{9,13},{10,... | collective-permute-start | bytes 393224 | tf_op jit(solution)/shard_map/ppermute | solution.py:22
  29.0 42.3 %collective-permute-start.5 = (bf16[128,512]{0,1:T(8,128)(2,1)}, bf16[128,512]{0,1:T(8,128)(2,1)}, u32[]{:S(2)}, u32[]{:S(2)}) collective-permute-start(bf16[128,512]{0,1:T(8,128)(2,1)} %get-tuple-element.19), channel_id=1, source_target_pairs={{0,3},{1,4},{2,5},{3,6},{4,7},{5,0},{6,1},{7,2},{8,11},{9,12},{10,... | collective-permute-start | bytes 393224 | tf_op jit(solution)/shard_map/ppermute | solution.py:22
  30.1 42.8 %collective-permute-start.6 = (bf16[128,512]{0,1:T(8,128)(2,1)}, bf16[128,512]{0,1:T(8,128)(2,1)S(1)}, u32[]{:S(2)}, u32[]{:S(2)}) collective-permute-start(bf16[128,512]{0,1:T(8,128)(2,1)} %get-tuple-element.18), channel_id=1, source_target_pairs={{0,2},{1,3},{2,4},{3,5},{4,6},{5,7},{6,0},{7,1},{8,10},{9,11},{10,... | collective-permute-start | bytes 393224 | tf_op jit(solution)/shard_map/ppermute | solution.py:22
  44.0 29.6 %collective-permute-start.7 = (bf16[128,512]{0,1:T(8,128)(2,1)}, bf16[128,512]{0,1:T(8,128)(2,1)S(1)}, u32[]{:S(2)}, u32[]{:S(2)}) collective-permute-start(bf16[128,512]{0,1:T(8,128)(2,1)} %get-tuple-element.17), channel_id=1, source_target_pairs={{0,1},{1,2},{2,3},{3,4},{4,5},{5,6},{6,7},{7,0},{8,9},{9,10},{10,1... | collective-permute-start | bytes 393224 | tf_op jit(solution)/shard_map/ppermute | solution.py:22
  80.8 11.5 %copy-start.11 = (s32[16,2]{0,1:T(2,128)S(1)}, s32[16,2]{0,1:T(2,128)}, u32[]{:S(2)}) copy-start(s32[16,2]{0,1:T(2,128)} %param.18) | copy-start | bytes 388
  80.8 43.4 %all-to-all-start.1 = ((bf16[128,8,512]{2,0,1:T(8,128)(2,1)}), bf16[128,8,512]{2,0,1:T(8,128)(2,1)}, u32[]{:S(2)}, u32[]{:S(2)}) async-start(bf16[128,8,512]{2,0,1:T(8,128)(2,1)} %bitcast.100), calls=%async_computation.1 | async-start | bytes 2097152 | tf_op jit(solution)/shard_map/all_to_all | solution.py:52
  87.8 9.2 %copy-start.2 = (bf16[1024,512]{0,1:T(8,128)(2,1)}, bf16[1024,512]{0,1:T(8,128)(2,1)S(1)}, u32[]{:S(2)}) copy-start(bf16[1024,512]{0,1:T(8,128)(2,1)S(1)} %constant_dynamic-slice_fusion) | copy-start | bytes 3145732
  87.9 26.3 %collective-permute-start.8 = (bf16[1024,512]{0,1:T(8,128)(2,1)S(1)}, bf16[1024,512]{0,1:T(8,128)(2,1)}, u32[]{:S(2)}, u32[]{:S(2)}) collective-permute-start(bf16[1024,512]{0,1:T(8,128)(2,1)S(1)} %constant_dynamic-slice_fusion), channel_id=1, source_target_pairs={{0,8},{8,16},{16,24},{1,9},{9,17},{17,25},{2,10},{10,18},{18,26},{... | collective-permute-start | bytes 3145736 | tf_op jit(solution)/shard_map/ppermute | solution.py:30
  118.6 26.9 %collective-permute-start = (bf16[1024,512]{0,1:T(8,128)(2,1)}, bf16[1024,512]{0,1:T(8,128)(2,1)}, u32[]{:S(2)}, u32[]{:S(2)}) collective-permute-start(bf16[1024,512]{0,1:T(8,128)(2,1)} %copy.51), channel_id=1, source_target_pairs={{0,8},{8,16},{16,24},{1,9},{9,17},{17,25},{2,10},{10,18},{18,26},{... | collective-permute-start | bytes 3145736 | tf_op jit(solution)/shard_map/ppermute | solution.py:30
  155.1 31.1 %all-to-all-start.2 = ((bf16[8,128,512]{2,1,0:T(8,128)(2,1)}), bf16[8,128,512]{2,1,0:T(8,128)(2,1)S(1)}, u32[]{:S(2)}, u32[]{:S(2)}) async-start(bf16[8,128,512]{2,1,0:T(8,128)(2,1)} %bitcast.23), calls=%async_computation.2 | async-start | bytes 2097152 | tf_op jit(solution)/shard_map/all_to_all | solution.py:101
  159.6 173.9 %all-gather.2.cloned.1.call-start = ((), (), s32[]{:S(2)}) async-start(), calls=%async_computation.6 | async-start | bytes 10485760 | tf_op jit(solution)/shard_map/all_gather | solution.py:125
  245.1 210.6 %reduce-scatter.2.cloned.1.call-start = ((), (), s32[]{:S(2)}) async-start(), calls=%async_computation.7 | async-start | bytes 10485760 | tf_op jit(solution)/shard_map/reduce_scatter | solution.py:133
  333.6 12.7 %copy-start.12 = (bf16[32,32,4096]{2,1,0:T(8,128)(2,1)S(1)}, bf16[32,32,4096]{2,1,0:T(8,128)(2,1)}, u32[]{:S(2)}) copy-start(bf16[32,32,4096]{2,1,0:T(8,128)(2,1)} %all-gather.2.cloned.1.call-done) | copy-start | bytes 25165828
  333.6 24.7 %slice-start = ((s8[8388608]{0:T(1024)(128)(4,1)}), s8[4194304]{0:T(1024)(128)(4,1)S(1)}, s32[]{:S(2)}) async-start(s8[8388608]{0:T(1024)(128)(4,1)} %bitcast.119), calls=%async_computation.8 | async-start | bytes 8388608
  346.3 12.0 %slice-start.1 = ((s8[8388608]{0:T(1024)(128)(4,1)}), s8[4194304]{0:T(1024)(128)(4,1)S(1)}, s32[]{:S(2)}) async-start(s8[8388608]{0:T(1024)(128)(4,1)} %bitcast.119), calls=%async_computation.9 | async-start | bytes 8388608
  369.3 91.4 %copy-start.10 = (f32[128,2]{0,1:T(2,128)S(1)}, f32[128,2]{0,1:T(2,128)}, u32[]{:S(2)}) copy-start(f32[128,2]{0,1:T(2,128)} %param.17) | copy-start | bytes 3076
  455.8 54.0 %all-to-all-start.4 = ((bf16[8,32,4096]{2,1,0:T(8,128)(2,1)}), bf16[8,32,4096]{2,1,0:T(8,128)(2,1)}, u32[]{:S(2)}, u32[]{:S(2)}) async-start(bf16[8,32,4096]{2,1,0:T(8,128)(2,1)} %reduce-scatter.2.cloned.1.call-done), calls=%async_computation.5 | async-start | bytes 4194304 | tf_op jit(solution)/shard_map/all_to_all | solution.py:136
  527.4 8.8 %copy-start.1 = (bf16[128,4096]{1,0:T(8,128)(2,1)S(1)}, bf16[128,4096]{1,0:T(8,128)(2,1)}, u32[]{:S(2)}) copy-start(bf16[128,4096]{1,0:T(8,128)(2,1)} %param.11) | copy-start | bytes 3145732
  (6 other events, 23.7 us)
Sparse Core Ops, SparseCore 0:
  245.3 88.2 all-gather.1
  369.4 86.3 reduce-scatter.1
